TPU v7x, 256 devices: a whole 4x4x8 slice. The times are simulated.
256 devices in a mesh: tp: 8 (over x, z_lo), wide: 32 (over y, z_hi, core).
Axes of the slice: x: 4, y: 4, z: 8 (z_hi: 4, z_lo: 2; z = z_hi * 2 + z_lo), core: 2. Of those that a mesh axis runs over, the one named last changes fastest.
Arguments:
- token_keys: bfloat16 [4096, 28672], P('tp', 'wide'), may hold values from -6 to 6
- resid_grad: bfloat16 [4096, 8192], P('wide', 'tp'), may hold values from -6 to 6
- kv_grad: bfloat16 [4096, 2048], P('wide', 'tp'), may hold values from -6 to 6
- kv_weight: bfloat16 [8192, 2048], P('wide', 'tp'), may hold values from -0.125 to 0.125
- editor_in: bfloat16 [8192, 1920], P('tp'), may hold values from -0.0625 to 0.0625
- editor_bias: float32 [1920], replicated, may hold values from -3 to 3
- editor_gain: float32 [8192], P('tp'), may hold values from 0.5 to 1.5
- editor_out: bfloat16 [1920, 8192], P(None, 'tp'), may hold values from -0.125 to 0.125
- prompt_len: int32 [64], replicated, may hold values from 1 to 63
Outputs:
- weight_update: bfloat16 [28672, 8192], P('wide', 'tp')
All inputs are finite; a program needn't handle non-finite values.
Results may differ from a plain program's by a relative error of at most 0.0055.
Values may be sent and summed in bfloat16 or wider, within the bound.
No kernel may reach another device: no remote copies, remote signals or barrier semaphores. Data moves between devices by JAX's collectives and lax.ppermute only.
A program may use at most 128 MiB of HBM per device.

v0:
```python
import jax
import jax.numpy as jnp
from jax import lax
from jax.sharding import PartitionSpec as P

LEN = 64
EPSILON = 1e-06


def per_device(
    token_keys,
    resid_grad,
    kv_grad,
    kv_weight,
    editor_in,
    editor_bias,
    editor_gain,
    editor_out,
    prompt_len,
):
    own_rows = resid_grad.shape[0]
    local_width = resid_grad.shape[1]
    col_start = lax.axis_index("tp") * local_width
    partial_sum = lax.dot_general(
        kv_grad,
        lax.all_gather(kv_weight, "wide", axis=0, tiled=True),
        (((1,), (1,)), ((), ())),
        preferred_element_type=jnp.float32,
    )
    resid_float = resid_grad.astype(jnp.float32)
    own_cols = lax.dynamic_slice_in_dim(partial_sum, col_start, local_width, 1) + resid_float
    partial_sum = lax.dynamic_update_slice_in_dim(partial_sum, own_cols, col_start, 1)
    complete = lax.psum(partial_sum, "tp")
    gradient = lax.dynamic_slice_in_dim(complete, col_start, local_width, 1)
    squares = jnp.sum(complete * complete, axis=1, keepdims=True)
    scaled = (gradient * editor_gain).astype(jnp.bfloat16)
    hidden_part = jnp.dot(scaled, editor_in, preferred_element_type=jnp.float32)
    projected = lax.psum(hidden_part, "tp")
    full_width = local_width * lax.axis_size("tp")
    inv_rms = lax.rsqrt(squares / full_width + EPSILON)
    hidden = jnp.maximum(projected * inv_rms + editor_bias, 0.0).astype(jnp.bfloat16)
    local_examples = own_rows // LEN
    owner_starts = lax.dynamic_slice_in_dim(
        prompt_len, lax.axis_index("wide") * local_examples, local_examples, 0
    )
    starts = jnp.repeat(owner_starts, LEN, total_repeat_length=own_rows)
    position = jnp.arange(own_rows, dtype=jnp.int32) % LEN
    keep_mask = (position >= starts).astype(jnp.float32)
    edited = (
        (gradient + jnp.dot(hidden, editor_out, preferred_element_type=jnp.float32))
        * keep_mask[:, None]
    ).astype(jnp.bfloat16)
    edit_count = jnp.sum(LEN - prompt_len).astype(jnp.float32)
    key_table = lax.all_gather(token_keys, "tp", axis=0, tiled=True)
    initial = jnp.zeros((key_table.shape[1], local_width), jnp.float32)
    piece = lax.all_gather(edited, "wide", axis=0, tiled=True)
    key_block = lax.slice_in_dim(key_table, 0, piece.shape[0], axis=0)
    summed = initial + lax.dot_general(
        key_block, piece, (((0,), (0,)), ((), ())), preferred_element_type=jnp.float32
    )
    return (summed * lax.rsqrt(edit_count)).astype(jnp.bfloat16)


def solution(mesh):
    in_specs = (
        P("tp", "wide"),
        P("wide", "tp"),
        P("wide", "tp"),
        P("wide", "tp"),
        P("tp", None),
        P(),
        P("tp"),
        P(None, "tp"),
        P(),
    )
    out_specs = P("wide", "tp")
    return jax.shard_map(
        per_device, mesh=mesh, in_specs=in_specs, out_specs=out_specs, check_vma=False
    )
```

profile of v0, /device:TPU:35, one launch (start us, length us, event | category | flops | bytes accessed | tf_op | source)
XLA Modules:
  0.0 611.1 jit_solution(15675389544332909423)
XLA Ops:
  6.5 0.0 copy-start
  6.5 0.0 all-gather.4.cloned.1.call-start
  6.5 0.7 all-gather.4.cloned.1.call-update
  7.3 0.0 all-reduce.3.cloned.1.call-start
  7.3 0.0 copy-start.1
  7.3 65.0 %all-gather.4.cloned.1.call-done = bf16[8192,256]{1,0:T(8,128)(2,1)} async-done(((bf16[256,256]{1,0:T(8,128)(2,1)}), bf16[8192,256]{1,0:T(8,128)(2,1)}) %all-gather.4.cloned.1.call-update) | async-done | bytes 4194320 | tf_op jit(solution)/shard_map/all_gather | solution.py:26
  72.4 0.0 copy-done
  72.4 5.6 fusion.11
  78.0 0.0 copy-done.1
  78.0 0.0 copy-start.3
  78.0 1.9 add_dynamic-update-slice_fusion
  80.0 0.0 all-reduce.3.cloned.1.call-update
  80.0 0.0 copy-start.5
  80.0 0.0 copy-start.4
  80.0 0.0 all-reduce.5.cloned.1.call-start
  80.1 185.2 %all-reduce.3.cloned.1.call-done = f32[128,8192]{1,0:T(8,128)} async-done(((f32[128,8192]{1,0:T(8,128)}), f32[128,8192]{1,0:T(8,128)}) %all-reduce.3.cloned.1.call-update) | async-done | bytes 4194320 | tf_op jit(solution)/shard_map/psum | solution.py:33
  265.3 0.0 copy-done.3
  265.3 4.0 fusion.6
  269.2 0.0 copy-start.2
  269.2 0.0 all-reduce.5.cloned.1.call-update
  269.3 0.0 all-gather.8.cloned.1.call-start
  269.3 0.5 all-gather.8.cloned.1.call-update
  269.8 0.0 all-gather.6.cloned.1.call-start
  269.9 0.0 copy-done.5
  269.9 0.1 dynamic_slice.11
  270.0 0.7 fusion.10
  270.6 0.0 copy-done.4
  270.6 1.3 compare_convert_fusion
  271.9 2.5 multiply_reduce_fusion
  274.5 73.6 %all-reduce.5.cloned.1.call-done = f32[128,1920]{1,0:T(8,128)} async-done(((f32[128,1920]{1,0:T(8,128)}), f32[128,1920]{1,0:T(8,128)}) %all-reduce.5.cloned.1.call-update) | async-done | bytes 983056 | tf_op jit(solution)/shard_map/psum | solution.py:38
  348.0 0.0 copy-done.2
  348.0 4.0 fusion.2
  352.0 0.0 all-gather.6.cloned.1.call-update
  352.1 0.6 subtract_reduce_fusion
  353.3 153.2 %all-gather.8.cloned.1.call-done = bf16[4096,896]{1,0:T(8,128)(2,1)} async-done(((bf16[512,896]{1,0:T(8,128)(2,1)}), bf16[4096,896]{1,0:T(8,128)(2,1)}) %all-gather.8.cloned.1.call-update) | async-done | bytes 7340048 | tf_op jit(solution)/shard_map/all_gather | solution.py:54
  506.5 82.3 %all-gather.6.cloned.1.call-done = bf16[4096,1024]{1,0:T(8,128)(2,1)} async-done(((bf16[128,1024]{1,0:T(8,128)(2,1)}), bf16[4096,1024]{1,0:T(8,128)(2,1)}) %all-gather.6.cloned.1.call-update) | async-done | bytes 8388624 | tf_op jit(solution)/shard_map/all_gather | solution.py:56
  588.8 13.4 %fusion = bf16[896,1024]{0,1:T(8,128)(2,1)S(1)} fusion(f32[]{:T(128)S(6)} %rsqrt.12, bf16[4096,1024]{1,0:T(8,128)(2,1)} %all-gather.6.cloned.1.call-done, bf16[4096,896]{1,0:T(8,128)(2,1)} %all-gather.8.cloned.1.call-done), kind=kOutput, calls=%fused_computation.2 | convolution fusion | flops 7518027776 | bytes 17563652 | tf_op jit(solution)/shard_map/dot_general | solution.py:58
  602.2 2.4 copy.10
  (1 shorter events, 0.0 us)
Async XLA Ops:
  6.5 65.8 %copy-start = (bf16[128,256]{1,0:T(8,128)(2,1)S(1)}, bf16[128,256]{1,0:T(8,128)(2,1)}, u32[]{:S(2)}) copy-start(bf16[128,256]{1,0:T(8,128)(2,1)} %param.13) | copy-start | bytes 196612
  6.5 65.8 %all-gather.4.cloned.1.call-start = ((), (), s32[]{:S(2)}) async-start(), calls=%async_computation | async-start | bytes 4325376 | tf_op jit(solution)/shard_map/all_gather | solution.py:26
  7.3 258.0 %all-reduce.3.cloned.1.call-start = ((), (), s32[]{:S(2)}) async-start(), calls=%async_computation.1 | async-start | bytes 8388608 | tf_op jit(solution)/shard_map/psum | solution.py:33
  7.3 70.7 %copy-start.1 = (bf16[128,1024]{1,0:T(8,128)(2,1)S(1)}, bf16[128,1024]{1,0:T(8,128)(2,1)}, u32[]{:S(2)}) copy-start(bf16[128,1024]{1,0:T(8,128)(2,1)} %param.12) | copy-start | bytes 786436
  78.0 187.2 %copy-start.3 = (f32[1024]{0:T(1024)S(1)}, f32[1024]{0:T(1024)}, u32[]{:S(2)}) copy-start(f32[1024]{0:T(1024)} %param.17) | copy-start | bytes 12292
  80.0 189.9 %copy-start.5 = (s32[64]{0:T(128)S(1)}, s32[64]{0:T(128)}, u32[]{:S(2)}) copy-start(s32[64]{0:T(128)} %param.19) | copy-start | bytes 772
  80.0 190.6 %copy-start.4 = (pred[128]{0:T(512)(128)(4,1)S(1)}, pred[128]{0:T(512)(128)(4,1)}, u32[]{:S(2)}) copy-start(pred[128]{0:T(512)(128)(4,1)} %constant.120) | copy-start | bytes 388
  80.0 268.0 %all-reduce.5.cloned.1.call-start = ((), (), s32[]{:S(2)}) async-start(), calls=%async_computation.2 | async-start | bytes 1966080 | tf_op jit(solution)/shard_map/psum | solution.py:38
  269.2 78.8 %copy-start.2 = (f32[1920]{0:T(1024)S(1)}, f32[1920]{0:T(1024)}, u32[]{:S(2)}) copy-start(f32[1920]{0:T(1024)} %param.16) | copy-start | bytes 23044
  269.3 237.3 %all-gather.8.cloned.1.call-start = ((), (), s32[]{:S(2)}) async-start(), calls=%async_computation.4 | async-start | bytes 8257536 | tf_op jit(solution)/shard_map/all_gather | solution.py:54
  269.8 318.9 %all-gather.6.cloned.1.call-start = ((), (), s32[]{:S(2)}) async-start(), calls=%async_computation.3 | async-start | bytes 8650752 | tf_op jit(solution)/shard_map/all_gather | solution.py:56
Sparse Core Ops, SparseCore 0:
  9.9 62.4 all-gather.3
  80.1 185.1 all-reduce.2
  269.4 78.6 all-reduce.4
  349.7 156.7 all-gather.7
  508.9 79.8 all-gather.5
where the time goes:
time: 611 us
  waiting for transfers between devices  561 us (92%)
  matrix products  27 us (4%)
  between operations  13.8 us (2%)
  other arithmetic  6.35 us (1%)
    psum x1, waiting for transfers between devices, per_device(): complete = lax.psum(partial_sum, 'tp')  185 us
    all_gather x1, waiting for transfers between devices, per_device(): key_table = lax.all_gather(token_keys, 'tp', axis=0, tiled=True)  153 us
    all_gather x1, waiting for transfers between devices, per_device(): piece = lax.all_gather(edited, 'wide', axis=0, tiled=True)  82.3 us
    psum x1, waiting for transfers between devices, per_device(): projected = lax.psum(hidden_part, 'tp')  73.6 us
    all_gather x1, waiting for transfers between devices, per_device(): lax.all_gather(kv_weight, 'wide', axis=0, tiled=True)  65 us
    dot_general x1, matrix products, per_device(): lax.dot_general(key_block, piece, (((0,), (0,)), ((), ())), preferred_ele...  13.4 us
  transfers between devices with their start and end apart: 5, of which 5 were waited for; matrix products, arithmetic and copies ran while one was open for 1% of the time, Pallas kernels for 0%

commit v1 on v0

--- a/solution.py
+++ b/solution.py
@@ -53,7 +53,9 @@
     edit_count = jnp.sum(LEN - prompt_len).astype(jnp.float32)
     key_table = lax.all_gather(token_keys, "tp", axis=0, tiled=True)
     initial = jnp.zeros((key_table.shape[1], local_width), jnp.float32)
-    piece = lax.all_gather(edited, "wide", axis=0, tiled=True)
+    piece = jnp.concatenate(
+        lax.all_to_all(jnp.stack([edited] * lax.axis_size("wide")), "wide", 0, 0), axis=0
+    )
     key_block = lax.slice_in_dim(key_table, 0, piece.shape[0], axis=0)
     summed = initial + lax.dot_general(
         key_block, piece, (((0,), (0,)), ((), ())), preferred_element_type=jnp.float32

time: 611 us -> 715 us (1.17)
  waiting for transfers between devices: 561 us -> 645 us
  starting transfers between devices: 0.16 us -> 13.3 us
    all_gather x1, waiting for transfers between devices: 153 us -> 320 us  [per_device(): key_table = lax.all_gather(token_keys, 'tp', axis=0, tiled=True)]
    all_gather x1 -> x0, waiting for transfers between devices: 82.3 us -> none  [per_device(): piece = lax.all_gather(edited, 'wide', axis=0, tiled=True)]
    all_to_all x0 -> x1, starting transfers between devices: none -> 13.1 us  [per_device(): lax.all_to_all(jnp.stack([edited] * lax.axis_size('wide')), 'wide', 0, 0)]
  transfers between devices with their start and end apart: 5 -> 5, of which waited for: 5 -> 4; matrix products, arithmetic and copies ran while one was open for 1% -> 1% of each run, Pallas kernels for 0% -> 0%
where the time goes in v1:
time: 715 us; the launch traced here: 713 us
  waiting for transfers between devices  645 us (90%)
  matrix products  26.3 us (4%)
  between operations  13.9 us (2%)
  starting transfers between devices  13.3 us (2%)
  local copies, waits for them, and re-layouts  7.42 us (1%)
    all_gather x1, waiting for transfers between devices, per_device(): key_table = lax.all_gather(token_keys, 'tp', axis=0, tiled=True)  320 us
    psum x1, waiting for transfers between devices, per_device(): complete = lax.psum(partial_sum, 'tp')  185 us
    psum x1, waiting for transfers between devices, per_device(): projected = lax.psum(hidden_part, 'tp')  74.3 us
    all_gather x1, waiting for transfers between devices, per_device(): lax.all_gather(kv_weight, 'wide', axis=0, tiled=True)  65 us
  transfers between devices with their start and end apart: 5, of which 4 were waited for; matrix products, arithmetic and copies ran while one was open for 1% of the time, Pallas kernels for 0%

profile of v1, /device:TPU:35, one launch (start us, length us, event | category | flops | bytes accessed | tf_op | source)
XLA Modules:
  0.0 712.6 jit_solution(2202960528107667863)
XLA Ops:
  6.5 0.0 copy-start
  6.5 0.0 all-gather.3.cloned.1.call-start
  6.5 0.7 all-gather.3.cloned.1.call-update
  7.3 0.0 all-reduce.3.cloned.1.call-start
  7.3 0.0 copy-start.1
  7.3 65.0 %all-gather.3.cloned.1.call-done = bf16[8192,256]{1,0:T(8,128)(2,1)} async-done(((bf16[256,256]{1,0:T(8,128)(2,1)}), bf16[8192,256]{1,0:T(8,128)(2,1)}) %all-gather.3.cloned.1.call-update) | async-done | bytes 4194320 | tf_op jit(solution)/shard_map/all_gather | solution.py:26
  72.4 0.0 copy-done
  72.4 5.7 fusion.11
  78.0 0.0 copy-done.1
  78.0 0.0 copy-start.3
  78.0 1.9 add_dynamic-update-slice_fusion
  79.9 0.0 all-reduce.3.cloned.1.call-update
  80.0 0.0 copy-start.5
  80.0 0.0 copy-start.4
  80.0 0.0 copy-start.2
  80.0 0.0 all-reduce.5.cloned.1.call-start
  80.1 185.2 %all-reduce.3.cloned.1.call-done = f32[128,8192]{1,0:T(8,128)} async-done(((f32[128,8192]{1,0:T(8,128)}), f32[128,8192]{1,0:T(8,128)}) %all-reduce.3.cloned.1.call-update) | async-done | bytes 4194320 | tf_op jit(solution)/shard_map/psum | solution.py:33
  265.2 0.0 copy-done.3
  265.2 4.0 fusion.6
  269.2 0.0 all-reduce.5.cloned.1.call-update
  269.2 0.0 copy-done.5
  269.2 0.1 dynamic_slice.11
  269.3 0.6 fusion.10
  269.9 0.0 copy-done.4
  269.9 1.3 compare_convert_fusion
  271.2 2.5 multiply_reduce_fusion
  273.7 74.3 %all-reduce.5.cloned.1.call-done = f32[128,1920]{1,0:T(8,128)} async-done(((f32[128,1920]{1,0:T(8,128)}), f32[128,1920]{1,0:T(8,128)}) %all-reduce.5.cloned.1.call-update) | async-done | bytes 983056 | tf_op jit(solution)/shard_map/psum | solution.py:38
  348.0 0.0 copy-done.2
  348.0 3.3 fusion.2
  351.3 4.3 stack.2
  355.6 13.1 %all-to-all-start = ((bf16[32,128,1024]{2,1,0:T(8,128)(2,1)}), bf16[32,128,1024]{2,1,0:T(8,128)(2,1)}, u32[]{:S(2)}, u32[]{:S(2)}) async-start(bf16[32,128,1024]{2,1,0:T(8,128)(2,1)} %stack.2), calls=%async_computation | async-start | bytes 16777216 | tf_op jit(solution)/shard_map/all_to_all | solution.py:57
  368.8 0.0 all-gather.5.cloned.1.call-start
  368.8 0.5 all-gather.5.cloned.1.call-update
  369.3 0.6 subtract_reduce_fusion
  370.7 319.6 %all-gather.5.cloned.1.call-done = bf16[4096,896]{1,0:T(8,128)(2,1)} async-done(((bf16[512,896]{1,0:T(8,128)(2,1)}), bf16[4096,896]{1,0:T(8,128)(2,1)}) %all-gather.5.cloned.1.call-update) | async-done | bytes 7340048 | tf_op jit(solution)/shard_map/all_gather | solution.py:54
  690.3 0.0 all-to-all-done
  690.3 13.4 %fusion = bf16[896,1024]{0,1:T(8,128)(2,1)S(1)} fusion(f32[]{:T(128)S(6)} %rsqrt.12, bf16[4096,1024]{1,0:T(8,128)(2,1)} %bitcast.2, bf16[4096,896]{1,0:T(8,128)(2,1)} %all-gather.5.cloned.1.call-done), kind=kOutput, calls=%fused_computation.2 | convolution fusion | flops 7518027776 | bytes 17563652 | tf_op jit(solution)/shard_map/dot_general | solution.py:60
  703.7 2.4 copy.10
  (1 shorter events, 0.0 us)
Async XLA Ops:
  6.5 65.8 %copy-start = (bf16[128,256]{1,0:T(8,128)(2,1)S(1)}, bf16[128,256]{1,0:T(8,128)(2,1)}, u32[]{:S(2)}) copy-start(bf16[128,256]{1,0:T(8,128)(2,1)} %param.13) | copy-start | bytes 196612
  6.5 65.8 %all-gather.3.cloned.1.call-start = ((), (), s32[]{:S(2)}) async-start(), calls=%async_computation.1 | async-start | bytes 4325376 | tf_op jit(solution)/shard_map/all_gather | solution.py:26
  7.3 258.0 %all-reduce.3.cloned.1.call-start = ((), (), s32[]{:S(2)}) async-start(), calls=%async_computation.2 | async-start | bytes 8388608 | tf_op jit(solution)/shard_map/psum | solution.py:33
  7.3 70.7 %copy-start.1 = (bf16[128,1024]{1,0:T(8,128)(2,1)S(1)}, bf16[128,1024]{1,0:T(8,128)(2,1)}, u32[]{:S(2)}) copy-start(bf16[128,1024]{1,0:T(8,128)(2,1)} %param.12) | copy-start | bytes 786436
  78.0 187.2 %copy-start.3 = (f32[1024]{0:T(1024)S(1)}, f32[1024]{0:T(1024)}, u32[]{:S(2)}) copy-start(f32[1024]{0:T(1024)} %param.17) | copy-start | bytes 12292
  80.0 189.3 %copy-start.5 = (s32[64]{0:T(128)S(1)}, s32[64]{0:T(128)}, u32[]{:S(2)}) copy-start(s32[64]{0:T(128)} %param.19) | copy-start | bytes 772
  80.0 189.9 %copy-start.4 = (pred[128]{0:T(512)(128)(4,1)S(1)}, pred[128]{0:T(512)(128)(4,1)}, u32[]{:S(2)}) copy-start(pred[128]{0:T(512)(128)(4,1)} %constant.120) | copy-start | bytes 388
  80.0 268.0 %copy-start.2 = (f32[1920]{0:T(1024)S(1)}, f32[1920]{0:T(1024)}, u32[]{:S(2)}) copy-start(f32[1920]{0:T(1024)} %param.16) | copy-start | bytes 23044
  80.0 268.0 %all-reduce.5.cloned.1.call-start = ((), (), s32[]{:S(2)}) async-start(), calls=%async_computation.3 | async-start | bytes 1966080 | tf_op jit(solution)/shard_map/psum | solution.py:38
  355.6 334.6 %all-to-all-start = ((bf16[32,128,1024]{2,1,0:T(8,128)(2,1)}), bf16[32,128,1024]{2,1,0:T(8,128)(2,1)}, u32[]{:S(2)}, u32[]{:S(2)}) async-start(bf16[32,128,1024]{2,1,0:T(8,128)(2,1)} %stack.2), calls=%async_computation | async-start | bytes 16777216 | tf_op jit(solution)/shard_map/all_to_all | solution.py:57
  368.8 321.5 %all-gather.5.cloned.1.call-start = ((), (), s32[]{:S(2)}) async-start(), calls=%async_computation.4 | async-start | bytes 8257536 | tf_op jit(solution)/shard_map/all_gather | solution.py:54
Sparse Core Ops, SparseCore 0:
  9.9 62.4 all-gather.2
  80.1 185.1 all-reduce.2
  269.3 78.6 all-reduce.4
  371.1 319.1 all-gather.4

commit v2 on v0

--- a/solution.py
+++ b/solution.py
@@ -35,7 +35,7 @@
     squares = jnp.sum(complete * complete, axis=1, keepdims=True)
     scaled = (gradient * editor_gain).astype(jnp.bfloat16)
     hidden_part = jnp.dot(scaled, editor_in, preferred_element_type=jnp.float32)
-    projected = lax.psum(hidden_part, "tp")
+    projected = jnp.sum(lax.all_gather(hidden_part, "tp"), axis=0)
     full_width = local_width * lax.axis_size("tp")
     inv_rms = lax.rsqrt(squares / full_width + EPSILON)
     hidden = jnp.maximum(projected * inv_rms + editor_bias, 0.0).astype(jnp.bfloat16)

time: 611 us -> 690 us (1.13)
  waiting for transfers between devices: 561 us -> 636 us
    all_gather x0 -> x1, waiting for transfers between devices: none -> 157 us  [per_device(): projected = jnp.sum(lax.all_gather(hidden_part, 'tp'), axis=0)]
    psum x1 -> x0, waiting for transfers between devices: 73.6 us -> none  [per_device(): projected = lax.psum(hidden_part, 'tp')]
    all_gather x1, waiting for transfers between devices: 153 us -> 145 us  [per_device(): key_table = lax.all_gather(token_keys, 'tp', axis=0, tiled=True)]
  transfers between devices with their start and end apart: 5 -> 5, of which waited for: 5 -> 5; matrix products, arithmetic and copies ran while one was open for 1% -> 2% of each run, Pallas kernels for 0% -> 0%
where the time goes in v2:
time: 690 us
  waiting for transfers between devices  636 us (92%)
  matrix products  26.7 us (4%)
  between operations  13.8 us (2%)
  other arithmetic  10.2 us (1%)
    psum x1, waiting for transfers between devices, per_device(): complete = lax.psum(partial_sum, 'tp')  185 us
    all_gather x1, waiting for transfers between devices, per_device(): projected = jnp.sum(lax.all_gather(hidden_part, 'tp'), axis=0)  157 us
    all_gather x1, waiting for transfers between devices, per_device(): key_table = lax.all_gather(token_keys, 'tp', axis=0, tiled=True)  145 us
    all_gather x1, waiting for transfers between devices, per_device(): piece = lax.all_gather(edited, 'wide', axis=0, tiled=True)  82.3 us
    all_gather x1, waiting for transfers between devices, per_device(): lax.all_gather(kv_weight, 'wide', axis=0, tiled=True)  65 us
  transfers between devices with their start and end apart: 5, of which 5 were waited for; matrix products, arithmetic and copies ran while one was open for 2% of the time, Pallas kernels for 0%

profile of v2, /device:TPU:35, one launch (start us, length us, event | category | flops | bytes accessed | tf_op | source)
XLA Modules:
  0.0 689.8 jit_solution(9113521425812279322)
XLA Ops:
  6.5 0.0 copy-start
  6.5 0.0 all-gather.6.cloned.1.call-start
  6.5 0.7 all-gather.6.cloned.1.call-update
  7.3 0.0 all-reduce.2.cloned.1.call-start
  7.3 0.0 copy-start.1
  7.3 65.0 %all-gather.6.cloned.1.call-done = bf16[8192,256]{1,0:T(8,128)(2,1)} async-done(((bf16[256,256]{1,0:T(8,128)(2,1)}), bf16[8192,256]{1,0:T(8,128)(2,1)}) %all-gather.6.cloned.1.call-update) | async-done | bytes 4194320 | tf_op jit(solution)/shard_map/all_gather | solution.py:26
  72.4 0.0 copy-done
  72.4 5.6 fusion.11
  78.0 0.0 copy-done.1
  78.0 0.0 copy-start.3
  78.0 1.9 add_dynamic-update-slice_fusion
  80.0 0.0 all-reduce.2.cloned.1.call-update
  80.0 0.0 copy-start.5
  80.0 0.0 copy-start.4
  80.0 0.0 all-gather.12.cloned.1.call-start
  80.0 185.2 %all-reduce.2.cloned.1.call-done = f32[128,8192]{1,0:T(8,128)} async-done(((f32[128,8192]{1,0:T(8,128)}), f32[128,8192]{1,0:T(8,128)}) %all-reduce.2.cloned.1.call-update) | async-done | bytes 4194320 | tf_op jit(solution)/shard_map/psum | solution.py:33
  265.2 0.0 copy-done.3
  265.2 4.0 fusion.6
  269.2 0.0 all-gather.12.cloned.1.call-update
  269.2 0.0 all-gather.10.cloned.1.call-start
  269.3 0.5 all-gather.10.cloned.1.call-update
  269.8 0.0 all-gather.8.cloned.1.call-start
  269.8 0.0 copy-done.5
  269.8 0.1 dynamic_slice.11
  269.9 0.7 fusion.10
  270.6 0.0 copy-done.4
  270.6 1.4 compare_convert_fusion
  272.0 2.5 multiply_reduce_fusion
  274.5 156.8 %all-gather.12.cloned.1.call-done = f32[1024,1920]{1,0:T(8,128)} async-done(((f32[128,1920]{1,0:T(8,128)}), f32[1024,1920]{1,0:T(8,128)}) %all-gather.12.cloned.1.call-update) | async-done | bytes 7864336 | tf_op jit(solution)/shard_map/all_gather | solution.py:38
  431.4 0.0 copy-start.2
  431.4 3.7 reduce_sum.27
  435.1 0.0 copy-done.2
  435.1 3.7 fusion.2
  438.8 0.0 all-gather.8.cloned.1.call-update
  438.8 0.6 subtract_reduce_fusion
  440.0 145.2 %all-gather.10.cloned.1.call-done = bf16[4096,896]{1,0:T(8,128)(2,1)} async-done(((bf16[512,896]{1,0:T(8,128)(2,1)}), bf16[4096,896]{1,0:T(8,128)(2,1)}) %all-gather.10.cloned.1.call-update) | async-done | bytes 7340048 | tf_op jit(solution)/shard_map/all_gather | solution.py:54
  585.2 82.3 %all-gather.8.cloned.1.call-done = bf16[4096,1024]{1,0:T(8,128)(2,1)} async-done(((bf16[128,1024]{1,0:T(8,128)(2,1)}), bf16[4096,1024]{1,0:T(8,128)(2,1)}) %all-gather.8.cloned.1.call-update) | async-done | bytes 8388624 | tf_op jit(solution)/shard_map/all_gather | solution.py:56
  667.5 13.4 %fusion = bf16[896,1024]{0,1:T(8,128)(2,1)S(1)} fusion(f32[]{:T(128)S(6)} %rsqrt.12, bf16[4096,1024]{1,0:T(8,128)(2,1)} %all-gather.8.cloned.1.call-done, bf16[4096,896]{1,0:T(8,128)(2,1)} %all-gather.10.cloned.1.call-done), kind=kOutput, calls=%fused_computation.2 | convolution fusion | flops 7518027776 | bytes 17563652 | tf_op jit(solution)/shard_map/dot_general | solution.py:58
  680.9 2.4 copy.10
  (1 shorter events, 0.0 us)
Async XLA Ops:
  6.5 65.8 %copy-start = (bf16[128,256]{1,0:T(8,128)(2,1)S(1)}, bf16[128,256]{1,0:T(8,128)(2,1)}, u32[]{:S(2)}) copy-start(bf16[128,256]{1,0:T(8,128)(2,1)} %param.13) | copy-start | bytes 196612
  6.5 65.8 %all-gather.6.cloned.1.call-start = ((), (), s32[]{:S(2)}) async-start(), calls=%async_computation | async-start | bytes 4325376 | tf_op jit(solution)/shard_map/all_gather | solution.py:26
  7.3 258.0 %all-reduce.2.cloned.1.call-start = ((), (), s32[]{:S(2)}) async-start(), calls=%async_computation.1 | async-start | bytes 8388608 | tf_op jit(solution)/shard_map/psum | solution.py:33
  7.3 70.7 %copy-start.1 = (bf16[128,1024]{1,0:T(8,128)(2,1)S(1)}, bf16[128,1024]{1,0:T(8,128)(2,1)}, u32[]{:S(2)}) copy-start(bf16[128,1024]{1,0:T(8,128)(2,1)} %param.12) | copy-start | bytes 786436
  78.0 187.2 %copy-start.3 = (f32[1024]{0:T(1024)S(1)}, f32[1024]{0:T(1024)}, u32[]{:S(2)}) copy-start(f32[1024]{0:T(1024)} %param.17) | copy-start | bytes 12292
  80.0 189.9 %copy-start.5 = (s32[64]{0:T(128)S(1)}, s32[64]{0:T(128)}, u32[]{:S(2)}) copy-start(s32[64]{0:T(128)} %param.19) | copy-start | bytes 772
  80.0 190.6 %copy-start.4 = (pred[128]{0:T(512)(128)(4,1)S(1)}, pred[128]{0:T(512)(128)(4,1)}, u32[]{:S(2)}) copy-start(pred[128]{0:T(512)(128)(4,1)} %constant.120) | copy-start | bytes 388
  80.0 351.4 %all-gather.12.cloned.1.call-start = ((), (), s32[]{:S(2)}) async-start(), calls=%async_computation.4 | async-start | bytes 8847360 | tf_op jit(solution)/shard_map/all_gather | solution.py:38
  269.2 316.0 %all-gather.10.cloned.1.call-start = ((), (), s32[]{:S(2)}) async-start(), calls=%async_computation.3 | async-start | bytes 8257536 | tf_op jit(solution)/shard_map/all_gather | solution.py:54
  269.8 397.7 %all-gather.8.cloned.1.call-start = ((), (), s32[]{:S(2)}) async-start(), calls=%async_computation.2 | async-start | bytes 8650752 | tf_op jit(solution)/shard_map/all_gather | solution.py:56
  431.4 3.7 copy-start.2
Sparse Core Ops, SparseCore 0:
  9.9 62.4 all-gather.5
  80.1 185.0 all-reduce.1
  269.3 161.9 all-gather.11
  433.0 152.1 all-gather.9
  587.6 79.8 all-gather.7
